TPU v7x, 512 devices: a whole 4x8x8 slice. The times are simulated.
512 devices in a mesh: panel: 2 (over y_lo), lon: 16 (over z, core), lat: 16 (over y_hi, x).
Axes of the slice: x: 4, y: 8 (y_hi: 4, y_lo: 2; y = y_hi * 2 + y_lo), z: 8, core: 2. Of those that a mesh axis runs over, the one named last changes fastest.
Arguments:
- pressure: float32 [2, 256, 512, 128], P('panel', 'lat', 'lon'), may hold values from -6 to 6
- porosity: float32 [2, 256, 512, 128], P('panel', 'lat', 'lon'), may hold values from 0.5 to 2
- source: float32 [2, 256, 512, 128], P('panel', 'lat', 'lon'), may hold values from -6 to 6
- bulk: float32 [2, 256, 512, 128], P('panel', 'lat', 'lon'), may hold values from 0.5 to 2
- lat_codes: int32 [2, 2, 2, 512], P('panel', None, None, 'lon'), may hold values from 0 to 8158, as said below
- lat_weights: float32 [2, 4, 2, 2, 512], P('panel', None, None, None, 'lon'), may hold values from 0 to 1, as said below
- lon_codes: int32 [2, 2, 2, 256], P('panel', None, None, 'lat'), may hold values from 0 to 8174, as said below
- lon_weights: float32 [2, 4, 2, 2, 256], P('panel', None, None, None, 'lat'), may hold values from 0 to 1, as said below
Outputs:
- pressure_out: float32 [2, 256, 512, 128], P('panel', 'lat', 'lon')
- porosity_out: float32 [2, 256, 512, 128], P('panel', 'lat', 'lon')
Inputs may be any that keep to these rules, and one draw needn't show every extreme that they name: `lat_codes`: an intersection map of the shell, which may differ from draw to draw: code = a * 32 + c with a < 255 a latitude of the whole panel and c < 31 an offset inside the longitude block of the ghost cell. `lon_codes`: an intersection map of the shell, which may differ from draw to draw: code = b * 16 + r with b < 511 a longitude of the whole panel and r < 15 an offset inside the latitude block of the ghost cell. `lat_weights`: the four weights of a ghost cell are non-negative and sum to one. `lon_weights`: the four weights of a ghost cell are non-negative and sum to one.
All inputs are finite; a program needn't handle non-finite values.
Results may differ from a plain program's by a relative error of at most 0.0003.
Values sent between devices are 32-bit elements; how exact they have to be, the bound alone decides.
A program may use at most 64 MiB of HBM per device.

v0:
```python
import jax
import jax.numpy as jnp
from jax import lax
from jax.sharding import PartitionSpec as P

SWEEPS = 3
stencil_offsets = ((0, 0), (0, 1), (1, 0), (1, 1))
radial_weight = 0.25
buoyancy = 0.5
time_step = 0.04


def padded_2(cells, sides, width):
    for axis, dim in sides:
        count = lax.axis_size(axis)
        ends = count - 1
        head = lax.slice_in_dim(cells, 0, width, axis=dim)
        tail = lax.slice_in_dim(cells, cells.shape[dim] - width, cells.shape[dim], axis=dim)
        cells = jnp.concatenate(
            [
                lax.ppermute(tail, axis, [(i, (i + 1) % count) for i in range(ends)]),
                cells,
                lax.ppermute(head, axis, [((i + 1) % count, i) for i in range(ends)]),
            ],
            axis=dim,
        )
    return cells


def swapped(block, axis, distance):
    count = lax.axis_size(axis)
    route = []
    for low in range(count):
        high = low | 1 << distance
        if high != low and high < count:
            route += [(low, high), (high, low)]
    return lax.ppermute(block, axis, route)


def pad_last(values, before, after):
    widths = [(0, 0)] * (values.ndim - 1) + [(before, after)]
    return jnp.pad(values, widths)


def rim_terms(field, lat_codes, lat_weights, lon_codes, lon_weights, width):
    rows_dev, cols_dev, levels = field.shape
    first_row = lax.axis_index("lat") * rows_dev
    first_col = lax.axis_index("lon") * cols_dev
    chosen = lat_codes[:, :width]
    rows_at = chosen // cols_dev - first_row
    cols_at = chosen % cols_dev
    lat_total = jnp.zeros(chosen.shape + (levels,), jnp.float32)
    for corner, (row_step, col_step) in enumerate(stencil_offsets):
        target = rows_at + row_step
        inside = (target >= 0) & (target < rows_dev)
        picked = field[jnp.clip(target, 0, rows_dev - 1), cols_at + col_step]
        lat_total = (
            lat_total + jnp.where(inside, lat_weights[corner, :, :width], 0.0)[..., None] * picked
        )
    chosen = lon_codes[:, :width]
    cols_at = chosen // rows_dev - first_col
    rows_at = chosen % rows_dev
    lon_total = jnp.zeros(chosen.shape + (levels,), jnp.float32)
    for corner, (row_step, col_step) in enumerate(stencil_offsets):
        target = cols_at + col_step
        inside = (target >= 0) & (target < cols_dev)
        picked = field[rows_at + row_step, jnp.clip(target, 0, cols_dev - 1)]
        lon_total = (
            lon_total + jnp.where(inside, lon_weights[corner, :, :width], 0.0)[..., None] * picked
        )
    return (lat_total, lon_total)


def surround(field, width, lat_codes, lat_weights, lon_codes, lon_weights):
    rows_dev, cols_dev, levels = field.shape
    padded = padded_2(field, (("lat", 0), ("lon", 1)), width)
    lat_terms, lon_terms = rim_terms(field, lat_codes, lat_weights, lon_codes, lon_weights, width)
    lat_summed = lax.psum(lat_terms, "lat")
    lon_summed = lax.psum(lon_terms, "lon")
    arrived = swapped(jnp.concatenate([lat_summed, lon_summed], axis=2), "panel", 0)
    lat_rim = arrived[:, :, :cols_dev]
    lon_rim = arrived[:, :, cols_dev:]
    lat_index = lax.axis_index("lat")
    lon_index = lax.axis_index("lon")
    last_lat = lax.axis_size("lat") - 1
    last_lon = lax.axis_size("lon") - 1
    north = jnp.where(lat_index == 0, lat_rim[0][::-1], padded[:width, width : width + cols_dev])
    padded = padded.at[:width, width : width + cols_dev].set(north)
    south = jnp.where(
        lat_index == last_lat, lat_rim[1], padded[width + rows_dev :, width : width + cols_dev]
    )
    padded = padded.at[width + rows_dev :, width : width + cols_dev].set(south)
    west = jnp.where(
        lon_index == 0,
        jnp.moveaxis(lon_rim[0][::-1], 0, 1),
        padded[width : width + rows_dev, :width],
    )
    padded = padded.at[width : width + rows_dev, :width].set(west)
    east = jnp.where(
        lon_index == last_lon,
        jnp.moveaxis(lon_rim[1], 0, 1),
        padded[width : width + rows_dev, width + cols_dev :],
    )
    padded = padded.at[width : width + rows_dev, width + cols_dev :].set(east)
    return padded


def face_terms(mobility):
    lat_face = 0.5 * (mobility[..., :-1, 1:-1, :] + mobility[..., 1:, 1:-1, :])
    lon_face = 0.5 * (mobility[..., 1:-1, :-1, :] + mobility[..., 1:-1, 1:, :])
    inner = mobility[..., 1:-1, 1:-1, :]
    mean_rad = 0.5 * (inner[..., :-1] + inner[..., 1:])
    return (lat_face, lon_face, mean_rad)


def diagonal_sum(bulk, lat_face, lon_face, mean_rad):
    rad_face = radial_weight * mean_rad
    total = bulk + lat_face[..., :-1, :, :] + lat_face[..., 1:, :, :]
    total = total + lon_face[..., :, :-1, :] + lon_face[..., :, 1:, :]
    return total + pad_last(rad_face, 1, 0) + pad_last(rad_face, 0, 1)


def neighbour_total(padded, source, lat_face, lon_face, mean_rad):
    inner = padded[..., 1:-1, 1:-1, :]
    rad_face = radial_weight * mean_rad
    total = source + lat_face[..., :-1, :, :] * padded[..., :-2, 1:-1, :]
    total = total + lat_face[..., 1:, :, :] * padded[..., 2:, 1:-1, :]
    total = total + lon_face[..., :, :-1, :] * padded[..., 1:-1, :-2, :]
    total = total + lon_face[..., :, 1:, :] * padded[..., 1:-1, 2:, :]
    total = (
        total
        + pad_last(rad_face * inner[..., :-1], 1, 0)
        + pad_last(rad_face * inner[..., 1:], 0, 1)
    )
    return total


def advect(pressure_pad, porosity_pad, lat_face, lon_face, mean_rad, bulk):
    pressure_in = pressure_pad[..., 1:-1, 1:-1, :]
    porosity_in = porosity_pad[..., 2:-2, 2:-2, :]
    lat_speed = -lat_face * (pressure_pad[..., 1:, 1:-1, :] - pressure_pad[..., :-1, 1:-1, :])
    lat_left = 1.5 * porosity_pad[..., 1:-2, 2:-2, :] - 0.5 * porosity_pad[..., :-3, 2:-2, :]
    lat_right = 1.5 * porosity_pad[..., 2:-1, 2:-2, :] - 0.5 * porosity_pad[..., 3:, 2:-2, :]
    lat_flux = lat_speed * jnp.where(lat_speed > 0, lat_left, lat_right)
    lon_speed = -lon_face * (pressure_pad[..., 1:-1, 1:, :] - pressure_pad[..., 1:-1, :-1, :])
    lon_left = 1.5 * porosity_pad[..., 2:-2, 1:-2, :] - 0.5 * porosity_pad[..., 2:-2, :-3, :]
    lon_right = 1.5 * porosity_pad[..., 2:-2, 2:-1, :] - 0.5 * porosity_pad[..., 2:-2, 3:, :]
    lon_flux = lon_speed * jnp.where(lon_speed > 0, lon_left, lon_right)
    rad_speed = (
        -radial_weight * mean_rad * (pressure_in[..., 1:] - pressure_in[..., :-1])
        + buoyancy * mean_rad
    )
    rad_flux = rad_speed * jnp.where(rad_speed > 0, porosity_in[..., :-1], porosity_in[..., 1:])
    divergence = lat_flux[..., 1:, :, :] - lat_flux[..., :-1, :, :]
    divergence = divergence + lon_flux[..., :, 1:, :] - lon_flux[..., :, :-1, :]
    divergence = divergence + pad_last(rad_flux, 0, 1) - pad_last(rad_flux, 1, 0)
    return porosity_in - time_step * (divergence + bulk * pressure_in)


def body(pressure, porosity, source, bulk, lat_codes, lat_weights, lon_codes, lon_weights):
    current = pressure[0]
    porosity_now = porosity[0]
    source_now = source[0]
    bulk_now = bulk[0]
    lat_code_now = lat_codes[0]
    lat_weight_now = lat_weights[0]
    lon_code_now = lon_codes[0]
    lon_weight_now = lon_weights[0]
    porosity_pad = surround(
        porosity_now, 2, lat_code_now, lat_weight_now, lon_code_now, lon_weight_now
    )
    near = porosity_pad[1:-1, 1:-1, :]
    mobility = near * near * near
    lat_face, lon_face, mean_rad = face_terms(mobility)
    denominator = diagonal_sum(bulk_now, lat_face, lon_face, mean_rad)
    for sweep_index in range(SWEEPS):
        padded = surround(current, 1, lat_code_now, lat_weight_now, lon_code_now, lon_weight_now)
        current = neighbour_total(padded, source_now, lat_face, lon_face, mean_rad) / denominator
    pressure_pad = surround(current, 1, lat_code_now, lat_weight_now, lon_code_now, lon_weight_now)
    porosity_new = advect(pressure_pad, porosity_pad, lat_face, lon_face, mean_rad, bulk_now)
    return (current[None], porosity_new[None])


def solution(mesh):
    placed = (
        P("panel", "lat", "lon", None),
        P("panel", "lat", "lon", None),
        P("panel", "lat", "lon", None),
        P("panel", "lat", "lon", None),
        P("panel", None, None, "lon"),
        P("panel", None, None, None, "lon"),
        P("panel", None, None, "lat"),
        P("panel", None, None, None, "lat"),
    )
    return jax.shard_map(
        body,
        mesh=mesh,
        in_specs=placed,
        out_specs=(P("panel", "lat", "lon", None), P("panel", "lat", "lon", None)),
        check_vma=False,
    )
```

profile of v0, /device:TPU:296, one launch (start us, length us, event | category | flops | bytes accessed | tf_op | source)
XLA Modules:
  0.0 695.2 jit_solution(16272074655665553990)
XLA Ops:
  14.9 3.5 collective-permute-start
  18.5 6.7 collective-permute-start.1
  36.6 76.8 %psum.72 = f32[2,1,32,128]{3,2,1,0:T(8,128)S(1)} all-reduce(f32[2,1,32,128]{3,2,1,0:T(8,128)S(1)} %multiply_add_fusion.4), channel_id=1, replica_groups=mesh['panel'=2,'lon'=16,'lat'=16] {'lat'}, use_global_device_ids=true, to_apply=%region_3.4 | all-reduce | flops 8192 | bytes 65536 | tf_op jit(solution)/shard_map/psum | solution.py:78
  113.6 47.4 %all-reduce.10 = (f32[2,1,16,128]{3,2,1,0:T(8,128)S(1)}, f32[2,2,16,128]{3,2,1,0:T(8,128)S(1)}) all-reduce(f32[2,1,16,128]{3,2,1,0:T(8,128)S(1)} %multiply_add_fusion.9, f32[2,2,16,128]{3,2,1,0:T(8,128)S(1)} %multiply_add_fusion.5), channel_id=1, replica_groups=mesh['panel'=2,'lon'=16,'lat'=16] {'lon'}, use_global_device_ids=true, to_apply=%region_4.5 | all-reduce | flops 12288 | bytes 98304 | tf_op jit(solution)/shard_map/psum | solution.py:79
  160.9 3.3 collective-permute-start.9
  166.2 8.1 %collective-permute-start.6 = (f32[1,32,128]{2,1,0:T(8,128)S(1)}, f32[1,32,128]{2,1,0:T(8,128)S(1)}, u32[]{:S(2)}, u32[]{:S(2)}) collective-permute-start(f32[1,32,128]{2,1,0:T(8,128)S(1)} %get-tuple-element.306), channel_id=1, source_target_pairs={{1,0},{2,1},{3,2},{4,3},{5,4},{6,5},{7,6},{8,7},{9,8},{10,9},{11,1... | collective-permute-start | bytes 49160 | tf_op jit(solution)/shard_map/ppermute | solution.py:23
  177.7 4.9 collective-permute-start.8
  185.9 4.9 collective-permute-start.3
  193.5 2.7 collective-permute-start.4
  196.3 3.7 collective-permute-done.4
  216.2 83.2 %psum.74 = f32[2,1,32,128]{3,2,1,0:T(8,128)S(1)} all-reduce(f32[2,1,32,128]{3,2,1,0:T(8,128)S(1)} %multiply_add_fusion.3), channel_id=1, replica_groups=mesh['panel'=2,'lon'=16,'lat'=16] {'lat'}, use_global_device_ids=true, to_apply=%region_5.6 | all-reduce | flops 8192 | bytes 65536 | tf_op jit(solution)/shard_map/psum | solution.py:78
  301.3 8.1 %collective-permute-start.11 = (f32[1,32,128]{2,0,1:T(1,128)S(1)}, f32[1,32,128]{2,0,1:T(1,128)S(1)}, u32[]{:S(2)}, u32[]{:S(2)}) collective-permute-start(f32[1,32,128]{2,0,1:T(1,128)S(1)} %slice.1292), channel_id=1, source_target_pairs={{1,0},{2,1},{3,2},{4,3},{5,4},{6,5},{7,6},{8,7},{9,8},{10,9},{11,1... | collective-permute-start | bytes 49160 | tf_op jit(solution)/shard_map/ppermute | solution.py:23
  309.5 45.7 %psum.75 = f32[2,1,16,128]{3,2,1,0:T(8,128)S(1)} all-reduce(f32[2,1,16,128]{3,2,1,0:T(8,128)S(1)} %multiply_add_fusion.8), channel_id=1, replica_groups=mesh['panel'=2,'lon'=16,'lat'=16] {'lon'}, use_global_device_ids=true, to_apply=%region_6.7 | all-reduce | flops 4096 | bytes 32768 | tf_op jit(solution)/shard_map/psum | solution.py:79
  357.2 4.9 collective-permute-start.13
  364.8 3.3 collective-permute-done.14
  378.7 76.9 %psum.76 = f32[2,1,32,128]{3,2,1,0:T(8,128)S(1)} all-reduce(f32[2,1,32,128]{3,2,1,0:T(8,128)S(1)} %multiply_add_fusion.2), channel_id=1, replica_groups=mesh['panel'=2,'lon'=16,'lat'=16] {'lat'}, use_global_device_ids=true, to_apply=%region_7.8 | all-reduce | flops 8192 | bytes 65536 | tf_op jit(solution)/shard_map/psum | solution.py:78
  457.5 8.1 %collective-permute-start.16 = (f32[1,32,128]{2,0,1:T(1,128)S(1)}, f32[1,32,128]{2,0,1:T(1,128)S(1)}, u32[]{:S(2)}, u32[]{:S(2)}) collective-permute-start(f32[1,32,128]{2,0,1:T(1,128)S(1)} %slice.1307), channel_id=1, source_target_pairs={{1,0},{2,1},{3,2},{4,3},{5,4},{6,5},{7,6},{8,7},{9,8},{10,9},{11,1... | collective-permute-start | bytes 49160 | tf_op jit(solution)/shard_map/ppermute | solution.py:23
  465.7 45.7 %psum.77 = f32[2,1,16,128]{3,2,1,0:T(8,128)S(1)} all-reduce(f32[2,1,16,128]{3,2,1,0:T(8,128)S(1)} %multiply_add_fusion.7), channel_id=1, replica_groups=mesh['panel'=2,'lon'=16,'lat'=16] {'lon'}, use_global_device_ids=true, to_apply=%region_8.9 | all-reduce | flops 4096 | bytes 32768 | tf_op jit(solution)/shard_map/psum | solution.py:79
  513.4 4.9 collective-permute-start.18
  520.8 3.5 collective-permute-done.19
  535.2 76.8 %psum.78 = f32[2,1,32,128]{3,2,1,0:T(8,128)S(1)} all-reduce(f32[2,1,32,128]{3,2,1,0:T(8,128)S(1)} %multiply_add_fusion.1), channel_id=1, replica_groups=mesh['panel'=2,'lon'=16,'lat'=16] {'lat'}, use_global_device_ids=true, to_apply=%region_9.10 | all-reduce | flops 8192 | bytes 65536 | tf_op jit(solution)/shard_map/psum | solution.py:78
  613.9 8.1 %collective-permute-start.21 = (f32[1,32,128]{2,0,1:T(1,128)S(1)}, f32[1,32,128]{2,0,1:T(1,128)S(1)}, u32[]{:S(2)}, u32[]{:S(2)}) collective-permute-start(f32[1,32,128]{2,0,1:T(1,128)S(1)} %slice.1323), channel_id=1, source_target_pairs={{1,0},{2,1},{3,2},{4,3},{5,4},{6,5},{7,6},{8,7},{9,8},{10,9},{11,1... | collective-permute-start | bytes 49160 | tf_op jit(solution)/shard_map/ppermute | solution.py:23
  622.1 45.7 %psum.79 = f32[2,1,16,128]{3,2,1,0:T(8,128)S(1)} all-reduce(f32[2,1,16,128]{3,2,1,0:T(8,128)S(1)} %multiply_add_fusion.6), channel_id=1, replica_groups=mesh['panel'=2,'lon'=16,'lat'=16] {'lon'}, use_global_device_ids=true, to_apply=%region_10.11 | all-reduce | flops 4096 | bytes 32768 | tf_op jit(solution)/shard_map/psum | solution.py:79
  669.8 4.9 collective-permute-start.23
  (292 shorter events, 98.0 us)
Async XLA Ops:
  7.2 185.5 %all-reduce.13.cloned.1.call-start = ((), (), s32[]{:S(2)}) async-start(), calls=%async_computation | async-start | bytes 131072 | tf_op jit(solution)/shard_map/psum | solution.py:78
  14.9 169.0 %collective-permute-start = (f32[2,32,128]{2,0,1:T(2,128)S(1)}, f32[2,32,128]{2,0,1:T(2,128)S(1)}, u32[]{:S(2)}, u32[]{:S(2)}) collective-permute-start(f32[2,32,128]{2,0,1:T(2,128)S(1)} %get-tuple-element.301), channel_id=1, source_target_pairs={{0,1},{1,2},{2,3},{3,4},{4,5},{5,6},{6,7},{7,8},{8,9},{9,10},{10,1... | collective-permute-start | bytes 98312 | tf_op jit(solution)/shard_map/ppermute | solution.py:21
  18.5 165.5 %collective-permute-start.1 = (f32[2,32,128]{2,0,1:T(2,128)S(1)}, f32[2,32,128]{2,0,1:T(2,128)S(1)}, u32[]{:S(2)}, u32[]{:S(2)}) collective-permute-start(f32[2,32,128]{2,0,1:T(2,128)S(1)} %get-tuple-element.302), channel_id=1, source_target_pairs={{1,0},{2,1},{3,2},{4,3},{5,4},{6,5},{7,6},{8,7},{9,8},{10,9},{11,1... | collective-permute-start | bytes 98312 | tf_op jit(solution)/shard_map/ppermute | solution.py:23
  160.9 29.8 %collective-permute-start.9 = (f32[2,1,48,128]{3,2,1,0:T(8,128)S(1)}, f32[2,1,48,128]{3,2,1,0:T(8,128)S(1)}, u32[]{:S(2)}, u32[]{:S(2)}) collective-permute-start(f32[2,1,48,128]{3,2,1,0:T(8,128)S(1)} %pad_maximum_fusion.6), channel_id=1, source_target_pairs={{0,256},{256,0},{1,257},{257,1},{2,258},{258,2},{3,259},{259,3},{4... | collective-permute-start | bytes 147464 | tf_op jit(solution)/shard_map/ppermute | solution.py:37
  164.2 11.5 %collective-permute-start.5 = (f32[1,32,128]{2,1,0:T(8,128)S(1)}, f32[1,32,128]{2,1,0:T(8,128)S(1)}, u32[]{:S(2)}, u32[]{:S(2)}) collective-permute-start(f32[1,32,128]{2,1,0:T(8,128)S(1)} %get-tuple-element.305), channel_id=1, source_target_pairs={{0,1},{1,2},{2,3},{3,4},{4,5},{5,6},{6,7},{7,8},{8,9},{9,10},{10,1... | collective-permute-start | bytes 49160 | tf_op jit(solution)/shard_map/ppermute | solution.py:21
  166.2 9.6 %collective-permute-start.6 = (f32[1,32,128]{2,1,0:T(8,128)S(1)}, f32[1,32,128]{2,1,0:T(8,128)S(1)}, u32[]{:S(2)}, u32[]{:S(2)}) collective-permute-start(f32[1,32,128]{2,1,0:T(8,128)S(1)} %get-tuple-element.306), channel_id=1, source_target_pairs={{1,0},{2,1},{3,2},{4,3},{5,4},{6,5},{7,6},{8,7},{9,8},{10,9},{11,1... | collective-permute-start | bytes 49160 | tf_op jit(solution)/shard_map/ppermute | solution.py:23
  175.8 7.4 %collective-permute-start.7 = (f32[18,1,128]{2,1,0:T(1,128)S(1)}, f32[18,1,128]{2,1,0:T(1,128)S(1)}, u32[]{:S(2)}, u32[]{:S(2)}) collective-permute-start(f32[18,1,128]{2,1,0:T(1,128)S(1)} %get-tuple-element.297), channel_id=1, source_target_pairs={{0,16},{16,32},{32,48},{48,64},{64,80},{80,96},{96,112},{112,128},... | collective-permute-start | bytes 27656 | tf_op jit(solution)/shard_map/ppermute | solution.py:21
  177.7 6.2 collective-permute-start.8
  184.0 12.2 %collective-permute-start.2 = (f32[20,2,128]{2,0,1:T(8,128)S(1)}, f32[20,2,128]{2,0,1:T(8,128)S(1)}, u32[]{:S(2)}, u32[]{:S(2)}) collective-permute-start(f32[20,2,128]{2,0,1:T(8,128)S(1)} %get-tuple-element.289), channel_id=1, source_target_pairs={{0,16},{16,32},{32,48},{48,64},{64,80},{80,96},{96,112},{112,128},... | collective-permute-start | bytes 61448 | tf_op jit(solution)/shard_map/ppermute | solution.py:21
  185.9 10.3 %collective-permute-start.3 = (f32[20,2,128]{2,0,1:T(8,128)S(1)}, f32[20,2,128]{2,0,1:T(8,128)S(1)}, u32[]{:S(2)}, u32[]{:S(2)}) collective-permute-start(f32[20,2,128]{2,0,1:T(8,128)S(1)} %get-tuple-element.290), channel_id=1, source_target_pairs={{16,0},{32,16},{48,32},{64,48},{80,64},{96,80},{112,96},{128,112},... | collective-permute-start | bytes 61448 | tf_op jit(solution)/shard_map/ppermute | solution.py:23
  193.5 6.5 collective-permute-start.4
  299.4 55.9 %collective-permute-start.10 = (f32[1,32,128]{2,1,0:T(8,128)S(1)}, f32[1,32,128]{2,1,0:T(8,128)S(1)}, u32[]{:S(2)}, u32[]{:S(2)}) collective-permute-start(f32[1,32,128]{2,1,0:T(8,128)S(1)} %slice.1291), channel_id=1, source_target_pairs={{0,1},{1,2},{2,3},{3,4},{4,5},{5,6},{6,7},{7,8},{8,9},{9,10},{10,1... | collective-permute-start | bytes 49160 | tf_op jit(solution)/shard_map/ppermute | solution.py:21
  301.3 54.0 %collective-permute-start.11 = (f32[1,32,128]{2,0,1:T(1,128)S(1)}, f32[1,32,128]{2,0,1:T(1,128)S(1)}, u32[]{:S(2)}, u32[]{:S(2)}) collective-permute-start(f32[1,32,128]{2,0,1:T(1,128)S(1)} %slice.1292), channel_id=1, source_target_pairs={{1,0},{2,1},{3,2},{4,3},{5,4},{6,5},{7,6},{8,7},{9,8},{10,9},{11,1... | collective-permute-start | bytes 49160 | tf_op jit(solution)/shard_map/ppermute | solution.py:23
  355.3 9.4 %collective-permute-start.12 = (f32[18,1,128]{2,0,1:T(8,128)S(1)}, f32[18,1,128]{2,0,1:T(8,128)S(1)}, u32[]{:S(2)}, u32[]{:S(2)}) collective-permute-start(f32[18,1,128]{2,0,1:T(8,128)S(1)} %get-tuple-element.295), channel_id=1, source_target_pairs={{0,16},{16,32},{32,48},{48,64},{64,80},{80,96},{96,112},{112,128},... | collective-permute-start | bytes 27656 | tf_op jit(solution)/shard_map/ppermute | solution.py:21
  357.2 7.5 %collective-permute-start.13 = (f32[18,1,128]{2,0,1:T(8,128)S(1)}, f32[18,1,128]{2,0,1:T(8,128)S(1)}, u32[]{:S(2)}, u32[]{:S(2)}) collective-permute-start(f32[18,1,128]{2,0,1:T(8,128)S(1)} %get-tuple-element.296), channel_id=1, source_target_pairs={{16,0},{32,16},{48,32},{64,48},{80,64},{96,80},{112,96},{128,112},... | collective-permute-start | bytes 27656 | tf_op jit(solution)/shard_map/ppermute | solution.py:23
  362.1 6.0 collective-permute-start.14
  455.6 55.9 %collective-permute-start.15 = (f32[1,32,128]{2,1,0:T(8,128)S(1)}, f32[1,32,128]{2,1,0:T(8,128)S(1)}, u32[]{:S(2)}, u32[]{:S(2)}) collective-permute-start(f32[1,32,128]{2,1,0:T(8,128)S(1)} %slice.1306), channel_id=1, source_target_pairs={{0,1},{1,2},{2,3},{3,4},{4,5},{5,6},{6,7},{7,8},{8,9},{9,10},{10,1... | collective-permute-start | bytes 49160 | tf_op jit(solution)/shard_map/ppermute | solution.py:21
  457.5 54.0 %collective-permute-start.16 = (f32[1,32,128]{2,0,1:T(1,128)S(1)}, f32[1,32,128]{2,0,1:T(1,128)S(1)}, u32[]{:S(2)}, u32[]{:S(2)}) collective-permute-start(f32[1,32,128]{2,0,1:T(1,128)S(1)} %slice.1307), channel_id=1, source_target_pairs={{1,0},{2,1},{3,2},{4,3},{5,4},{6,5},{7,6},{8,7},{9,8},{10,9},{11,1... | collective-permute-start | bytes 49160 | tf_op jit(solution)/shard_map/ppermute | solution.py:23
  511.5 9.2 %collective-permute-start.17 = (f32[18,1,128]{2,0,1:T(8,128)S(1)}, f32[18,1,128]{2,0,1:T(8,128)S(1)}, u32[]{:S(2)}, u32[]{:S(2)}) collective-permute-start(f32[18,1,128]{2,0,1:T(8,128)S(1)} %get-tuple-element.293), channel_id=1, source_target_pairs={{0,16},{16,32},{32,48},{48,64},{64,80},{80,96},{96,112},{112,128},... | collective-permute-start | bytes 27656 | tf_op jit(solution)/shard_map/ppermute | solution.py:21
  513.4 7.3 %collective-permute-start.18 = (f32[18,1,128]{2,0,1:T(8,128)S(1)}, f32[18,1,128]{2,0,1:T(8,128)S(1)}, u32[]{:S(2)}, u32[]{:S(2)}) collective-permute-start(f32[18,1,128]{2,0,1:T(8,128)S(1)} %get-tuple-element.294), channel_id=1, source_target_pairs={{16,0},{32,16},{48,32},{64,48},{80,64},{96,80},{112,96},{128,112},... | collective-permute-start | bytes 27656 | tf_op jit(solution)/shard_map/ppermute | solution.py:23
  611.9 55.9 %collective-permute-start.20 = (f32[1,32,128]{2,1,0:T(8,128)S(1)}, f32[1,32,128]{2,1,0:T(8,128)S(1)}, u32[]{:S(2)}, u32[]{:S(2)}) collective-permute-start(f32[1,32,128]{2,1,0:T(8,128)S(1)} %slice.1322), channel_id=1, source_target_pairs={{0,1},{1,2},{2,3},{3,4},{4,5},{5,6},{6,7},{7,8},{8,9},{9,10},{10,1... | collective-permute-start | bytes 49160 | tf_op jit(solution)/shard_map/ppermute | solution.py:21
  613.9 54.0 %collective-permute-start.21 = (f32[1,32,128]{2,0,1:T(1,128)S(1)}, f32[1,32,128]{2,0,1:T(1,128)S(1)}, u32[]{:S(2)}, u32[]{:S(2)}) collective-permute-start(f32[1,32,128]{2,0,1:T(1,128)S(1)} %slice.1323), channel_id=1, source_target_pairs={{1,0},{2,1},{3,2},{4,3},{5,4},{6,5},{7,6},{8,7},{9,8},{10,9},{11,1... | collective-permute-start | bytes 49160 | tf_op jit(solution)/shard_map/ppermute | solution.py:23
  667.9 10.0 %collective-permute-start.22 = (f32[18,1,128]{2,0,1:T(8,128)S(1)}, f32[18,1,128]{2,0,1:T(8,128)S(1)}, u32[]{:S(2)}, u32[]{:S(2)}) collective-permute-start(f32[18,1,128]{2,0,1:T(8,128)S(1)} %get-tuple-element.291), channel_id=1, source_target_pairs={{0,16},{16,32},{32,48},{48,64},{64,80},{80,96},{96,112},{112,128},... | collective-permute-start | bytes 27656 | tf_op jit(solution)/shard_map/ppermute | solution.py:21
  669.8 8.1 %collective-permute-start.23 = (f32[18,1,128]{2,0,1:T(8,128)S(1)}, f32[18,1,128]{2,0,1:T(8,128)S(1)}, u32[]{:S(2)}, u32[]{:S(2)}) collective-permute-start(f32[18,1,128]{2,0,1:T(8,128)S(1)} %get-tuple-element.292), channel_id=1, source_target_pairs={{16,0},{32,16},{48,32},{64,48},{80,64},{96,80},{112,96},{128,112},... | collective-permute-start | bytes 27656 | tf_op jit(solution)/shard_map/ppermute | solution.py:23
  (26 other events, 79.8 us)
Sparse Core Ops, SparseCore 0:
  14.8 158.6 all-reduce.12
where the time goes:
time: 696 us; the launch traced here: 695 us
  blocking collectives  498 us (72%)
  starting transfers between devices  97.7 us (14%)
  local copies, waits for them, and re-layouts  57.8 us (8%)
  between operations  15.5 us (2%)
  waiting for transfers between devices  13.9 us (2%)
  other arithmetic  12 us (2%)
    psum x4, blocking collectives, surround(): lat_summed = lax.psum(lat_terms, 'lat')  314 us
    psum x4, blocking collectives, surround(): lon_summed = lax.psum(lon_terms, 'lon')  185 us
    ppermute x10, starting transfers between devices, padded_2(): lax.ppermute(head, axis, [((i + 1) % count, i) for i in range(ends)])  63.5 us
    ppermute x10, starting transfers between devices, padded_2(): lax.ppermute(tail, axis, [(i, (i + 1) % count) for i in range(ends)])  20.8 us
    gather x20, local copies, waits for them, and re-layouts, rim_terms(): picked = field[jnp.clip(target, 0, rows_dev - 1), cols_at + col_step]  19.7 us
    gather x20, local copies, waits for them, and re-layouts, rim_terms(): picked = field[rows_at + row_step, jnp.clip(target, 0, cols_dev - 1)]  14.8 us
  transfers between devices with their start and end apart: 26, of which 5 were waited for; matrix products, arithmetic and copies ran while one was open for 3% of the time, Pallas kernels for 0%

commit v1 on v0

--- a/solution.py
+++ b/solution.py
@@ -75,7 +75,8 @@
     rows_dev, cols_dev, levels = field.shape
     padded = padded_2(field, (("lat", 0), ("lon", 1)), width)
     lat_terms, lon_terms = rim_terms(field, lat_codes, lat_weights, lon_codes, lon_weights, width)
-    lat_summed = lax.psum(lat_terms, "lat")
+    t_next = lax.all_gather(lat_terms, "lat")
+    lat_summed = jnp.sum(t_next, axis=0)
     lon_summed = lax.psum(lon_terms, "lon")
     arrived = swapped(jnp.concatenate([lat_summed, lon_summed], axis=2), "panel", 0)
     lat_rim = arrived[:, :, :cols_dev]

time: 696 us -> 583 us (0.84)
  the two profiles are of different devices: /device:TPU:296 before, /device:TPU:288 now
where the time goes in v1:
time: 583 us; the launch traced here: 582 us
  blocking collectives  356 us (61%)
  starting transfers between devices  96.2 us (17%)
  local copies, waits for them, and re-layouts  56.2 us (10%)
  waiting for transfers between devices  41.9 us (7%)
  other arithmetic  15.8 us (3%)
  between operations  15.5 us (3%)
    psum x4, blocking collectives, surround(): lon_summed = lax.psum(lon_terms, 'lon')  183 us
    all_gather x4, blocking collectives, surround(): t_next = lax.all_gather(lat_terms, 'lat')  173 us
    ppermute x10, starting transfers between devices, padded_2(): lax.ppermute(head, axis, [((i + 1) % count, i) for i in range(ends)])  63.1 us
    all_gather x1, waiting for transfers between devices, surround(): t_next = lax.all_gather(lat_terms, 'lat')  26.4 us
    ppermute x10, starting transfers between devices, padded_2(): lax.ppermute(tail, axis, [(i, (i + 1) % count) for i in range(ends)])  21 us
    gather x20, local copies, waits for them, and re-layouts, rim_terms(): picked = field[jnp.clip(target, 0, rows_dev - 1), cols_at + col_step]  19 us
    gather x20, local copies, waits for them, and re-layouts, rim_terms(): picked = field[rows_at + row_step, jnp.clip(target, 0, cols_dev - 1)]  15.7 us
    ppermute x5, waiting for transfers between devices, swapped(): return lax.ppermute(block, axis, route)  14.7 us
  transfers between devices with their start and end apart: 26, of which 6 were waited for; matrix products, arithmetic and copies ran while one was open for 2% of the time, Pallas kernels for 0%

profile of v1, /device:TPU:288, one launch (start us, length us, event | category | flops | bytes accessed | tf_op | source)
XLA Modules:
  0.0 581.9 jit_solution(17447674924875510925)
XLA Ops:
  23.2 43.9 %all_gather.21 = f32[16,2,1,32,128]{4,3,2,1,0:T(8,128)S(1)} all-gather(f32[1,2,1,32,128]{4,3,2,1,0:T(8,128)S(1)} %multiply_add_fusion.4), channel_id=1, replica_groups=mesh['panel'=2,'lon'=16,'lat'=16] {'lat'}, dimensions={0}, use_global_device_ids=true | all-gather | bytes 557056 | tf_op jit(solution)/shard_map/all_gather | solution.py:78
  67.3 45.8 %all-reduce.10 = (f32[2,2,16,128]{3,2,1,0:T(8,128)S(1)}, f32[2,1,16,128]{3,2,1,0:T(8,128)S(1)}) all-reduce(f32[2,2,16,128]{3,2,1,0:T(8,128)S(1)} %multiply_add_fusion.5, f32[2,1,16,128]{3,2,1,0:T(8,128)S(1)} %multiply_add_fusion.9), channel_id=1, replica_groups=mesh['panel'=2,'lon'=16,'lat'=16] {'lon'}, use_global_device_ids=true, to_apply=%region_2.3 | all-reduce | flops 12288 | bytes 98304 | tf_op jit(solution)/shard_map/psum | solution.py:80
  113.1 3.8 collective-permute-start.9
  118.8 8.1 %collective-permute-start.6 = (f32[1,32,128]{2,1,0:T(8,128)S(1)}, f32[1,32,128]{2,1,0:T(8,128)S(1)}, u32[]{:S(2)}, u32[]{:S(2)}) collective-permute-start(f32[1,32,128]{2,1,0:T(8,128)S(1)} %get-tuple-element.292), channel_id=1, source_target_pairs={{1,0},{2,1},{3,2},{4,3},{5,4},{6,5},{7,6},{8,7},{9,8},{10,9},{11,1... | collective-permute-start | bytes 49160 | tf_op jit(solution)/shard_map/ppermute | solution.py:23
  135.1 8.1 %collective-permute-start.1 = (f32[2,32,128]{2,1,0:T(8,128)S(1)}, f32[2,32,128]{2,1,0:T(8,128)S(1)}, u32[]{:S(2)}, u32[]{:S(2)}) collective-permute-start(f32[2,32,128]{2,1,0:T(8,128)S(1)} %get-tuple-element.290), channel_id=1, source_target_pairs={{1,0},{2,1},{3,2},{4,3},{5,4},{6,5},{7,6},{8,7},{9,8},{10,9},{11,1... | collective-permute-start | bytes 98312 | tf_op jit(solution)/shard_map/ppermute | solution.py:23
  146.6 4.9 collective-permute-start.8
  154.8 4.9 collective-permute-start.3
  161.6 26.4 %all-gather.2.cloned.1.call-done = f32[16,2,2,32,128]{4,3,2,1,0:T(8,128)} async-done(((f32[1,2,2,32,128]{4,3,2,1,0:T(8,128)}), f32[16,2,2,32,128]{4,3,2,1,0:T(8,128)}) %all-gather.2.cloned.1.call-update) | async-done | bytes 1048592 | tf_op jit(solution)/shard_map/all_gather | solution.py:78
  209.5 45.7 %all_gather.22 = f32[16,2,1,32,128]{4,3,2,1,0:T(8,128)S(1)} all-gather(f32[1,2,1,32,128]{4,3,2,1,0:T(8,128)S(1)} %multiply_add_fusion.3), channel_id=1, replica_groups=mesh['panel'=2,'lon'=16,'lat'=16] {'lat'}, dimensions={0}, use_global_device_ids=true | all-gather | bytes 557056 | tf_op jit(solution)/shard_map/all_gather | solution.py:78
  257.1 8.1 %collective-permute-start.11 = (f32[1,32,128]{2,0,1:T(1,128)}, f32[1,32,128]{2,0,1:T(1,128)S(1)}, u32[]{:S(2)}, u32[]{:S(2)}) collective-permute-start(f32[1,32,128]{2,0,1:T(1,128)} %slice.1290), channel_id=1, source_target_pairs={{1,0},{2,1},{3,2},{4,3},{5,4},{6,5},{7,6},{8,7},{9,8},{10,9},{11,1... | collective-permute-start | bytes 49160 | tf_op jit(solution)/shard_map/ppermute | solution.py:23
  266.7 45.7 %psum.37 = f32[2,1,16,128]{3,2,1,0:T(8,128)S(1)} all-reduce(f32[2,1,16,128]{3,2,1,0:T(8,128)S(1)} %multiply_add_fusion.8), channel_id=1, replica_groups=mesh['panel'=2,'lon'=16,'lat'=16] {'lon'}, use_global_device_ids=true, to_apply=%region_6.7 | all-reduce | flops 4096 | bytes 32768 | tf_op jit(solution)/shard_map/psum | solution.py:80
  314.4 4.9 collective-permute-start.13
  321.3 4.0 collective-permute-done.14
  337.4 42.4 %all_gather.23 = f32[16,2,1,32,128]{4,3,2,1,0:T(8,128)S(1)} all-gather(f32[1,2,1,32,128]{4,3,2,1,0:T(8,128)S(1)} %multiply_add_fusion.2), channel_id=1, replica_groups=mesh['panel'=2,'lon'=16,'lat'=16] {'lat'}, dimensions={0}, use_global_device_ids=true | all-gather | bytes 557056 | tf_op jit(solution)/shard_map/all_gather | solution.py:78
  382.2 7.7 %collective-permute-start.16 = (f32[1,32,128]{2,0,1:T(1,128)}, f32[1,32,128]{2,0,1:T(1,128)S(1)}, u32[]{:S(2)}, u32[]{:S(2)}) collective-permute-start(f32[1,32,128]{2,0,1:T(1,128)} %slice.1305), channel_id=1, source_target_pairs={{1,0},{2,1},{3,2},{4,3},{5,4},{6,5},{7,6},{8,7},{9,8},{10,9},{11,1... | collective-permute-start | bytes 49160 | tf_op jit(solution)/shard_map/ppermute | solution.py:23
  391.4 45.7 %psum.38 = f32[2,1,16,128]{3,2,1,0:T(8,128)S(1)} all-reduce(f32[2,1,16,128]{3,2,1,0:T(8,128)S(1)} %multiply_add_fusion.7), channel_id=1, replica_groups=mesh['panel'=2,'lon'=16,'lat'=16] {'lon'}, use_global_device_ids=true, to_apply=%region_8.9 | all-reduce | flops 4096 | bytes 32768 | tf_op jit(solution)/shard_map/psum | solution.py:80
  439.1 4.9 collective-permute-start.18
  445.9 4.0 collective-permute-done.19
  460.8 41.4 %all_gather.24 = f32[16,2,1,32,128]{4,3,2,1,0:T(8,128)S(1)} all-gather(f32[1,2,1,32,128]{4,3,2,1,0:T(8,128)S(1)} %multiply_add_fusion.1), channel_id=1, replica_groups=mesh['panel'=2,'lon'=16,'lat'=16] {'lat'}, dimensions={0}, use_global_device_ids=true | all-gather | bytes 557056 | tf_op jit(solution)/shard_map/all_gather | solution.py:78
  502.2 3.3 collective-permute-start.20
  505.5 6.8 %collective-permute-start.21 = (f32[1,32,128]{2,1,0:T(8,128)S(1)}, f32[1,32,128]{2,1,0:T(8,128)S(1)}, u32[]{:S(2)}, u32[]{:S(2)}) collective-permute-start(f32[1,32,128]{2,1,0:T(8,128)S(1)} %get-tuple-element.288), channel_id=1, source_target_pairs={{1,0},{2,1},{3,2},{4,3},{5,4},{6,5},{7,6},{8,7},{9,8},{10,9},{11,1... | collective-permute-start | bytes 49160 | tf_op jit(solution)/shard_map/ppermute | solution.py:23
  513.1 45.7 %psum.39 = f32[2,1,16,128]{3,2,1,0:T(8,128)S(1)} all-reduce(f32[2,1,16,128]{3,2,1,0:T(8,128)S(1)} %multiply_add_fusion.6), channel_id=1, replica_groups=mesh['panel'=2,'lon'=16,'lat'=16] {'lon'}, use_global_device_ids=true, to_apply=%region_10.11 | all-reduce | flops 4096 | bytes 32768 | tf_op jit(solution)/shard_map/psum | solution.py:80
  560.8 4.9 collective-permute-start.23
  567.7 4.0 collective-permute-done.24
  (305 shorter events, 101.6 us)
Async XLA Ops:
  7.2 180.8 %all-gather.2.cloned.1.call-start = ((), (), s32[]{:S(2)}) async-start(), calls=%async_computation | async-start | bytes 1114112 | tf_op jit(solution)/shard_map/all_gather | solution.py:78
  113.1 46.6 %collective-permute-start.9 = (f32[2,1,48,128]{3,2,1,0:T(8,128)S(1)}, f32[2,1,48,128]{3,2,1,0:T(8,128)S(1)}, u32[]{:S(2)}, u32[]{:S(2)}) collective-permute-start(f32[2,1,48,128]{3,2,1,0:T(8,128)S(1)} %pad_maximum_fusion.6), channel_id=1, source_target_pairs={{0,256},{256,0},{1,257},{257,1},{2,258},{258,2},{3,259},{259,3},{4... | collective-permute-start | bytes 147464 | tf_op jit(solution)/shard_map/ppermute | solution.py:37
  116.9 27.7 %collective-permute-start.5 = (f32[1,32,128]{2,1,0:T(8,128)S(1)}, f32[1,32,128]{2,1,0:T(8,128)S(1)}, u32[]{:S(2)}, u32[]{:S(2)}) collective-permute-start(f32[1,32,128]{2,1,0:T(8,128)S(1)} %get-tuple-element.291), channel_id=1, source_target_pairs={{0,1},{1,2},{2,3},{3,4},{4,5},{5,6},{6,7},{7,8},{8,9},{9,10},{10,1... | collective-permute-start | bytes 49160 | tf_op jit(solution)/shard_map/ppermute | solution.py:21
  118.8 25.8 %collective-permute-start.6 = (f32[1,32,128]{2,1,0:T(8,128)S(1)}, f32[1,32,128]{2,1,0:T(8,128)S(1)}, u32[]{:S(2)}, u32[]{:S(2)}) collective-permute-start(f32[1,32,128]{2,1,0:T(8,128)S(1)} %get-tuple-element.292), channel_id=1, source_target_pairs={{1,0},{2,1},{3,2},{4,3},{5,4},{6,5},{7,6},{8,7},{9,8},{10,9},{11,1... | collective-permute-start | bytes 49160 | tf_op jit(solution)/shard_map/ppermute | solution.py:23
  133.1 19.7 %collective-permute-start = (f32[2,32,128]{2,0,1:T(2,128)S(1)}, f32[2,32,128]{2,0,1:T(2,128)S(1)}, u32[]{:S(2)}, u32[]{:S(2)}) collective-permute-start(f32[2,32,128]{2,0,1:T(2,128)S(1)} %bitcast.440), channel_id=1, source_target_pairs={{0,1},{1,2},{2,3},{3,4},{4,5},{5,6},{6,7},{7,8},{8,9},{9,10},{10,1... | collective-permute-start | bytes 98312 | tf_op jit(solution)/shard_map/ppermute | solution.py:21
  135.1 17.8 %collective-permute-start.1 = (f32[2,32,128]{2,1,0:T(8,128)S(1)}, f32[2,32,128]{2,1,0:T(8,128)S(1)}, u32[]{:S(2)}, u32[]{:S(2)}) collective-permute-start(f32[2,32,128]{2,1,0:T(8,128)S(1)} %get-tuple-element.290), channel_id=1, source_target_pairs={{1,0},{2,1},{3,2},{4,3},{5,4},{6,5},{7,6},{8,7},{9,8},{10,9},{11,1... | collective-permute-start | bytes 98312 | tf_op jit(solution)/shard_map/ppermute | solution.py:23
  144.7 7.4 %collective-permute-start.7 = (f32[18,1,128]{2,1,0:T(1,128)S(1)}, f32[18,1,128]{2,1,0:T(1,128)S(1)}, u32[]{:S(2)}, u32[]{:S(2)}) collective-permute-start(f32[18,1,128]{2,1,0:T(1,128)S(1)} %get-tuple-element.283), channel_id=1, source_target_pairs={{0,16},{16,32},{32,48},{48,64},{64,80},{80,96},{96,112},{112,128},... | collective-permute-start | bytes 27656 | tf_op jit(solution)/shard_map/ppermute | solution.py:21
  146.6 6.2 %collective-permute-start.8 = (f32[18,1,128]{2,1,0:T(1,128)S(1)}, f32[18,1,128]{2,1,0:T(1,128)S(1)}, u32[]{:S(2)}, u32[]{:S(2)}) collective-permute-start(f32[18,1,128]{2,1,0:T(1,128)S(1)} %get-tuple-element.284), channel_id=1, source_target_pairs={{16,0},{32,16},{48,32},{64,48},{80,64},{96,80},{112,96},{128,112},... | collective-permute-start | bytes 27656 | tf_op jit(solution)/shard_map/ppermute | solution.py:23
  152.9 8.6 %collective-permute-start.2 = (f32[20,2,128]{2,1,0:T(2,128)S(1)}, f32[20,2,128]{2,1,0:T(2,128)S(1)}, u32[]{:S(2)}, u32[]{:S(2)}) collective-permute-start(f32[20,2,128]{2,1,0:T(2,128)S(1)} %get-tuple-element.275), channel_id=1, source_target_pairs={{0,16},{16,32},{32,48},{48,64},{64,80},{80,96},{96,112},{112,128},... | collective-permute-start | bytes 61448 | tf_op jit(solution)/shard_map/ppermute | solution.py:21
  154.8 6.7 %collective-permute-start.3 = (f32[20,2,128]{2,1,0:T(2,128)S(1)}, f32[20,2,128]{2,1,0:T(2,128)S(1)}, u32[]{:S(2)}, u32[]{:S(2)}) collective-permute-start(f32[20,2,128]{2,1,0:T(2,128)S(1)} %get-tuple-element.276), channel_id=1, source_target_pairs={{16,0},{32,16},{48,32},{64,48},{80,64},{96,80},{112,96},{128,112},... | collective-permute-start | bytes 61448 | tf_op jit(solution)/shard_map/ppermute | solution.py:23
  189.4 6.5 %collective-permute-start.4 = (f32[2,2,48,128]{3,1,2,0:T(2,128)S(1)}, f32[2,2,48,128]{3,1,2,0:T(2,128)S(1)}, u32[]{:S(2)}, u32[]{:S(2)}) collective-permute-start(f32[2,2,48,128]{3,1,2,0:T(2,128)S(1)} %pad_maximum_fusion.5), channel_id=1, source_target_pairs={{0,256},{256,0},{1,257},{257,1},{2,258},{258,2},{3,259},{259,3},{4... | collective-permute-start | bytes 294920 | tf_op jit(solution)/shard_map/ppermute | solution.py:37
  255.2 57.3 %collective-permute-start.10 = (f32[1,32,128]{2,1,0:T(8,128)}, f32[1,32,128]{2,1,0:T(8,128)S(1)}, u32[]{:S(2)}, u32[]{:S(2)}) collective-permute-start(f32[1,32,128]{2,1,0:T(8,128)} %slice.1289), channel_id=1, source_target_pairs={{0,1},{1,2},{2,3},{3,4},{4,5},{5,6},{6,7},{7,8},{8,9},{9,10},{10,1... | collective-permute-start | bytes 49160 | tf_op jit(solution)/shard_map/ppermute | solution.py:21
  257.1 55.3 %collective-permute-start.11 = (f32[1,32,128]{2,0,1:T(1,128)}, f32[1,32,128]{2,0,1:T(1,128)S(1)}, u32[]{:S(2)}, u32[]{:S(2)}) collective-permute-start(f32[1,32,128]{2,0,1:T(1,128)} %slice.1290), channel_id=1, source_target_pairs={{1,0},{2,1},{3,2},{4,3},{5,4},{6,5},{7,6},{8,7},{9,8},{10,9},{11,1... | collective-permute-start | bytes 49160 | tf_op jit(solution)/shard_map/ppermute | solution.py:23
  312.5 8.7 %collective-permute-start.12 = (f32[18,1,128]{2,0,1:T(8,128)S(1)}, f32[18,1,128]{2,0,1:T(8,128)S(1)}, u32[]{:S(2)}, u32[]{:S(2)}) collective-permute-start(f32[18,1,128]{2,0,1:T(8,128)S(1)} %get-tuple-element.281), channel_id=1, source_target_pairs={{0,16},{16,32},{32,48},{48,64},{64,80},{80,96},{96,112},{112,128},... | collective-permute-start | bytes 27656 | tf_op jit(solution)/shard_map/ppermute | solution.py:21
  314.4 6.8 %collective-permute-start.13 = (f32[18,1,128]{2,0,1:T(8,128)S(1)}, f32[18,1,128]{2,0,1:T(8,128)S(1)}, u32[]{:S(2)}, u32[]{:S(2)}) collective-permute-start(f32[18,1,128]{2,0,1:T(8,128)S(1)} %get-tuple-element.282), channel_id=1, source_target_pairs={{16,0},{32,16},{48,32},{64,48},{80,64},{96,80},{112,96},{128,112},... | collective-permute-start | bytes 27656 | tf_op jit(solution)/shard_map/ppermute | solution.py:23
  379.8 57.3 %collective-permute-start.15 = (f32[1,32,128]{2,1,0:T(8,128)}, f32[1,32,128]{2,1,0:T(8,128)S(1)}, u32[]{:S(2)}, u32[]{:S(2)}) collective-permute-start(f32[1,32,128]{2,1,0:T(8,128)} %slice.1304), channel_id=1, source_target_pairs={{0,1},{1,2},{2,3},{3,4},{4,5},{5,6},{6,7},{7,8},{8,9},{9,10},{10,1... | collective-permute-start | bytes 49160 | tf_op jit(solution)/shard_map/ppermute | solution.py:21
  382.2 54.9 %collective-permute-start.16 = (f32[1,32,128]{2,0,1:T(1,128)}, f32[1,32,128]{2,0,1:T(1,128)S(1)}, u32[]{:S(2)}, u32[]{:S(2)}) collective-permute-start(f32[1,32,128]{2,0,1:T(1,128)} %slice.1305), channel_id=1, source_target_pairs={{1,0},{2,1},{3,2},{4,3},{5,4},{6,5},{7,6},{8,7},{9,8},{10,9},{11,1... | collective-permute-start | bytes 49160 | tf_op jit(solution)/shard_map/ppermute | solution.py:23
  437.1 8.7 %collective-permute-start.17 = (f32[18,1,128]{2,0,1:T(8,128)S(1)}, f32[18,1,128]{2,0,1:T(8,128)S(1)}, u32[]{:S(2)}, u32[]{:S(2)}) collective-permute-start(f32[18,1,128]{2,0,1:T(8,128)S(1)} %get-tuple-element.279), channel_id=1, source_target_pairs={{0,16},{16,32},{32,48},{48,64},{64,80},{80,96},{96,112},{112,128},... | collective-permute-start | bytes 27656 | tf_op jit(solution)/shard_map/ppermute | solution.py:21
  439.1 6.8 %collective-permute-start.18 = (f32[18,1,128]{2,0,1:T(8,128)S(1)}, f32[18,1,128]{2,0,1:T(8,128)S(1)}, u32[]{:S(2)}, u32[]{:S(2)}) collective-permute-start(f32[18,1,128]{2,0,1:T(8,128)S(1)} %get-tuple-element.280), channel_id=1, source_target_pairs={{16,0},{32,16},{48,32},{64,48},{80,64},{96,80},{112,96},{128,112},... | collective-permute-start | bytes 27656 | tf_op jit(solution)/shard_map/ppermute | solution.py:23
  443.9 6.0 %collective-permute-start.19 = (f32[2,1,48,128]{3,2,1,0:T(8,128)S(1)}, f32[2,1,48,128]{3,2,1,0:T(8,128)S(1)}, u32[]{:S(2)}, u32[]{:S(2)}) collective-permute-start(f32[2,1,48,128]{3,2,1,0:T(8,128)S(1)} %pad_maximum_fusion.8), channel_id=1, source_target_pairs={{0,256},{256,0},{1,257},{257,1},{2,258},{258,2},{3,259},{259,3},{4... | collective-permute-start | bytes 147464 | tf_op jit(solution)/shard_map/ppermute | solution.py:37
  502.2 56.6 %collective-permute-start.20 = (f32[1,32,128]{2,1,0:T(8,128)S(1)}, f32[1,32,128]{2,1,0:T(8,128)S(1)}, u32[]{:S(2)}, u32[]{:S(2)}) collective-permute-start(f32[1,32,128]{2,1,0:T(8,128)S(1)} %get-tuple-element.287), channel_id=1, source_target_pairs={{0,1},{1,2},{2,3},{3,4},{4,5},{5,6},{6,7},{7,8},{8,9},{9,10},{10,1... | collective-permute-start | bytes 49160 | tf_op jit(solution)/shard_map/ppermute | solution.py:21
  505.5 53.3 %collective-permute-start.21 = (f32[1,32,128]{2,1,0:T(8,128)S(1)}, f32[1,32,128]{2,1,0:T(8,128)S(1)}, u32[]{:S(2)}, u32[]{:S(2)}) collective-permute-start(f32[1,32,128]{2,1,0:T(8,128)S(1)} %get-tuple-element.288), channel_id=1, source_target_pairs={{1,0},{2,1},{3,2},{4,3},{5,4},{6,5},{7,6},{8,7},{9,8},{10,9},{11,1... | collective-permute-start | bytes 49160 | tf_op jit(solution)/shard_map/ppermute | solution.py:23
  558.9 8.7 %collective-permute-start.22 = (f32[18,1,128]{2,1,0:T(1,128)S(1)}, f32[18,1,128]{2,1,0:T(1,128)S(1)}, u32[]{:S(2)}, u32[]{:S(2)}) collective-permute-start(f32[18,1,128]{2,1,0:T(1,128)S(1)} %get-tuple-element.277), channel_id=1, source_target_pairs={{0,16},{16,32},{32,48},{48,64},{64,80},{80,96},{96,112},{112,128},... | collective-permute-start | bytes 27656 | tf_op jit(solution)/shard_map/ppermute | solution.py:21
  560.8 6.8 %collective-permute-start.23 = (f32[18,1,128]{2,1,0:T(1,128)S(1)}, f32[18,1,128]{2,1,0:T(1,128)S(1)}, u32[]{:S(2)}, u32[]{:S(2)}) collective-permute-start(f32[18,1,128]{2,1,0:T(1,128)S(1)} %get-tuple-element.278), channel_id=1, source_target_pairs={{16,0},{32,16},{48,32},{64,48},{80,64},{96,80},{112,96},{128,112},... | collective-permute-start | bytes 27656 | tf_op jit(solution)/shard_map/ppermute | solution.py:23
  (30 other events, 1035.1 us)
Sparse Core Ops, SparseCore 0:
  133.2 54.7 all-gather.1
